TPU v7x, 32 devices: a whole 2x2x4 slice. The times are simulated.
32 devices in a mesh: pipe: 1, expert: 32 (over z, y, x, core).
Axes of the slice: x: 2, y: 2, z: 4, core: 2. Of those that a mesh axis runs over, the one named last changes fastest.
Arguments:
- inputs: bfloat16 [1, 2, 2048, 2048], P('pipe', None, 'expert'), may hold values from -6 to 6
- grads_out: bfloat16 [1, 2, 2048, 2048], P('pipe', None, 'expert'), may hold values from -6 to 6
- expert_ids: int32 [1, 2, 2048, 6], P('pipe', None, 'expert'), may hold values from 0 to 31, all different within a row; in each aligned block of 64 rows (0 to 63, 64 to 127, ..., all dimensions but the last counted through in order) at most 32 rows name the same one
- gate_values: float32 [1, 2, 2048, 6], P('pipe', None, 'expert'), may hold values from 0.1 to 0.5
- w_gate: bfloat16 [1, 32, 2048, 768], P('pipe', 'expert'), may hold values from -0.125 to 0.125
- w_up: bfloat16 [1, 32, 2048, 768], P('pipe', 'expert'), may hold values from -0.125 to 0.125
- w_down: bfloat16 [1, 32, 768, 2048], P('pipe', 'expert'), may hold values from -0.21875 to 0.21875
Outputs:
- received: bfloat16 [1, 2, 2048, 2048], P('pipe', None, 'expert')
- gate_grad: float32 [1, 2, 2048, 6], P('pipe', None, 'expert')
Inputs may be any that keep to these rules, and one draw needn't show every extreme that they name: `expert_ids`: each row names 6 different experts. Within the 64 rows of one device for one section and micro-batch, no expert is named by more than 32 rows, a bound that some expert reaches in some of these blocks.
All inputs are finite; a program needn't handle non-finite values.
Results may differ from a plain program's by a relative error of at most 0.0041.
Values may be sent and summed in bfloat16 or wider, within the bound.
A program may use at most 128 MiB of HBM per device.

v0:
```python
import jax
import jax.numpy as jnp
from jax import lax
from jax.sharding import PartitionSpec as P


def shortened(array):
    return jax.tree.map(lambda a: a.astype(jnp.bfloat16) if a.dtype == jnp.float32 else a, array)


def from_behind(value, axis, steps):
    count = lax.axis_size(axis)
    pairs = [(source, (source + steps) % count) for source in range(count)]
    return lax.ppermute(value, axis, pairs)


def expert_rows(x_rows, grad_rows, gate_weight, up_weight, down_weight):
    gate_pre = jnp.dot(x_rows, gate_weight, preferred_element_type=jnp.float32)
    up_pre = jnp.dot(x_rows, up_weight, preferred_element_type=jnp.float32)
    back_grad = lax.dot_general(
        grad_rows, down_weight, (((1,), (1,)), ((), ())), preferred_element_type=jnp.float32
    )
    logistic = jax.nn.sigmoid(gate_pre)
    swish = gate_pre * logistic
    score = jnp.sum(back_grad * swish * up_pre, axis=1).astype(jnp.bfloat16)
    d_gate = (back_grad * up_pre * logistic * (1.0 + gate_pre * (1.0 - logistic))).astype(
        jnp.bfloat16
    )
    d_up = (back_grad * swish).astype(jnp.bfloat16)
    pair_grad = lax.dot_general(
        d_gate, gate_weight, (((1,), (1,)), ((), ())), preferred_element_type=jnp.float32
    )
    pair_grad = pair_grad + lax.dot_general(
        d_up, up_weight, (((1,), (1,)), ((), ())), preferred_element_type=jnp.float32
    )
    return (pair_grad.astype(jnp.bfloat16), score)


def slot_table(ids_group, experts, capacity):
    groups, rows, picks = ids_group.shape
    flat_ids = ids_group.reshape(groups, rows * picks)
    onehot = (flat_ids[:, :, None] == jnp.arange(experts, dtype=jnp.int32)[None, None, :]).astype(
        jnp.int32
    )
    earlier = jnp.cumsum(onehot, axis=1) - onehot
    position = jnp.sum(earlier * onehot, axis=2)
    counts = jnp.sum(onehot, axis=1)
    group_index = jnp.arange(groups, dtype=jnp.int32)[:, None]
    target = flat_ids * (groups * capacity) + group_index * capacity + position
    return (target.reshape(-1), counts)


def expert_pass(x_group, grad_group, ids_group, seen, weights, send, bring_back, capacity):
    experts = seen.shape[0]
    groups, rows, width = x_group.shape
    picks = ids_group.shape[2]
    target, unused_counts = slot_table(ids_group, experts, capacity)
    total = experts * groups * capacity
    token_of = jnp.arange(groups * rows * picks, dtype=jnp.int32) // picks
    x_flat = x_group.reshape(groups * rows, width)
    grad_flat = grad_group.reshape(groups * rows, width)
    send_x = jnp.zeros((total, width), jnp.bfloat16).at[target].set(x_flat[token_of])
    send_grad = jnp.zeros((total, width), jnp.bfloat16).at[target].set(grad_flat[token_of])
    got_x, got_grad = send(
        (
            send_x.reshape(experts, groups * capacity, width),
            send_grad.reshape(experts, groups * capacity, width),
        )
    )
    slot = jnp.arange(groups * capacity, dtype=jnp.int32)
    limit = seen[:, slot // capacity]
    live = ((slot % capacity)[None, :] < limit).reshape(-1)
    block = min(256, total)
    padded = (total + block - 1) // block * block
    order = jnp.cumsum(live.astype(jnp.int32)) - 1
    used = jnp.sum(live.astype(jnp.int32))
    place = jnp.where(live, order, padded)
    pack_x = (
        jnp.zeros((padded, width), jnp.bfloat16)
        .at[place]
        .set(got_x.reshape(total, width), mode="drop")
    )
    pack_grad = (
        jnp.zeros((padded, width), jnp.bfloat16)
        .at[place]
        .set(got_grad.reshape(total, width), mode="drop")
    )
    gate_weight, up_weight, down_weight = weights

    def one_block(index, carry):
        block_grads, block_scores = carry
        start = index * block
        grad_rows, score_rows = expert_rows(
            lax.dynamic_slice_in_dim(pack_x, start, block, 0),
            lax.dynamic_slice_in_dim(pack_grad, start, block, 0),
            gate_weight,
            up_weight,
            down_weight,
        )
        return (
            lax.dynamic_update_slice_in_dim(block_grads, grad_rows, start, 0),
            lax.dynamic_update_slice_in_dim(block_scores, score_rows, start, 0),
        )

    empty = (jnp.zeros((padded, width), jnp.bfloat16), jnp.zeros((padded,), jnp.bfloat16))
    block_grads, block_scores = lax.fori_loop(0, (used + block - 1) // block, one_block, empty)
    source = jnp.minimum(place, padded - 1)
    out_rows = jnp.where(live[:, None], block_grads[source], jnp.zeros((), jnp.bfloat16))
    out_scores = jnp.where(live, block_scores[source], jnp.zeros((), jnp.bfloat16))
    ret_rows, ret_scores = bring_back(
        (
            out_rows.reshape(experts, groups * capacity, width),
            out_scores.reshape(experts, groups * capacity),
        )
    )
    pair_grad = ret_rows.reshape(total, width)[target].reshape(groups, rows, picks, width)
    pair_score = ret_scores.reshape(total)[target].reshape(groups, rows, picks)
    return (pair_grad, pair_score)


def on_device(inputs, grads_out, expert_ids, gate_values, w_gate, w_up, w_down):
    experts = lax.axis_size("expert")
    self_index = lax.axis_index("expert")
    x_all = inputs[0]
    grad_all = grads_out[0]
    ids_all = expert_ids[0]
    gates_all = gate_values[0]
    micro_count, rows, width = x_all.shape
    picks = ids_all.shape[2]
    capacity = min(rows, 8 * rows * picks // (3 * experts))
    unused_target, local_counts = slot_table(ids_all, experts, capacity)
    table = lax.all_gather(local_counts[None], "expert", axis=0, tiled=True)
    seen = jnp.take(table, self_index, axis=2)
    weights = (w_gate[0, 0], w_up[0, 0], w_down[0, 0])
    delivered = []
    scores = []

    def send_each(pair):
        return jax.tree.map(
            lambda part, own: part.astype(own.dtype),
            lax.all_to_all(shortened(pair), "expert", split_axis=0, concat_axis=0, tiled=True),
            pair,
        )

    def back_each(pair):
        return jax.tree.map(
            lambda part, own: part.astype(own.dtype),
            lax.all_to_all(shortened(pair), "expert", split_axis=0, concat_axis=0, tiled=True),
            pair,
        )

    for micro in range(micro_count):
        pair_grad, pair_score = expert_pass(
            x_all[micro : micro + 1],
            grad_all[micro : micro + 1],
            ids_all[micro : micro + 1],
            seen[:, micro : micro + 1],
            weights,
            send_each,
            back_each,
            capacity,
        )
        gates_part = gates_all[micro : micro + 1]
        combined = grad_all[micro : micro + 1].astype(jnp.float32) + jnp.sum(
            gates_part[..., None] * pair_grad.astype(jnp.float32), axis=2
        )
        moved = combined.astype(jnp.bfloat16)[None]
        score_part = pair_score.astype(jnp.float32)
        delivered.append(moved)
        scores.append(score_part)
    received = jnp.concatenate(delivered, axis=1)
    received = from_behind(received, "pipe", -1)
    gate_grad = jnp.concatenate(scores, axis=0)[None]
    return (received, gate_grad)


def solution(mesh):
    placed = (
        P("pipe", None, "expert", None),
        P("pipe", None, "expert", None),
        P("pipe", None, "expert", None),
        P("pipe", None, "expert", None),
        P("pipe", "expert", None, None),
        P("pipe", "expert", None, None),
        P("pipe", "expert", None, None),
    )
    return jax.shard_map(
        on_device,
        mesh=mesh,
        in_specs=placed,
        out_specs=(P("pipe", None, "expert", None), P("pipe", None, "expert", None)),
        check_vma=False,
    )
```

profile of v0, /device:TPU:8, one launch (start us, length us, event | category | flops | bytes accessed | tf_op | source)
XLA Modules:
  0.0 718.6 jit_solution(1070911775478979147)
XLA Ops:
  4.4 10.5 %scatter_custom_fusion = bf16[1024,2048]{1,0:T(8,128)(2,1)} fusion(s32[384]{0:T(512)S(1)} %fusion.59, bf16[]{:T(256)} %constant.139.clone.1, bf16[64,2048]{1,0:T(8,128)(2,1)S(1)} %get-tuple-element.165, s32[1024]{0:T(1024)S(1)} %pad_clamp_fusion.2), kind=kCustom, calls=%fused_computation.78 | custom fusion | bytes 4194306 | tf_op jit(solution)/shard_map/scatter | solution.py:63
  14.9 6.8 all-to-all-start
  21.8 10.5 %scatter_custom_fusion.2 = bf16[1024,2048]{1,0:T(8,128)(2,1)} fusion(s32[384]{0:T(512)S(1)} %fusion.59, bf16[]{:T(256)} %constant.139.clone.1, bf16[64,2048]{1,0:T(8,128)(2,1)S(1)} %get-tuple-element.163, s32[1024]{0:T(1024)S(1)} %pad_clamp_fusion.2), kind=kCustom, calls=%fused_computation.74 | custom fusion | bytes 4194306 | tf_op jit(solution)/shard_map/scatter | solution.py:62
  32.2 80.7 %all-to-all-done = bf16[32,32,2048]{2,1,0:T(8,128)(2,1)} async-done(((bf16[32,32,2048]{2,1,0:T(8,128)(2,1)}), bf16[32,32,2048]{2,1,0:T(8,128)(2,1)}, u32[]{:S(2)}, u32[]{:S(2)}) %all-to-all-start) | async-done | bytes 4194336 | tf_op jit(solution)/shard_map/all_to_all | solution.py:141
  112.9 6.9 all-to-all-start.1
  121.7 10.4 %scatter_custom_fusion.4 = bf16[1024,2048]{1,0:T(8,128)(2,1)} fusion(s32[384]{0:T(512)S(1)} %fusion.61, bf16[]{:T(256)} %constant.139.clone.1, bf16[64,2048]{1,0:T(8,128)(2,1)S(1)} %get-tuple-element.166, s32[1024]{0:T(1024)S(1)} %pad_clamp_fusion.2), kind=kCustom, calls=%fused_computation.70 | custom fusion | bytes 4194306 | tf_op jit(solution)/shard_map/scatter | solution.py:63
  132.2 78.9 %all-to-all-done.1 = bf16[32,32,2048]{2,1,0:T(8,128)(2,1)} async-done(((bf16[32,32,2048]{2,1,0:T(8,128)(2,1)}), bf16[32,32,2048]{2,1,0:T(8,128)(2,1)}, u32[]{:S(2)}, u32[]{:S(2)}) %all-to-all-start.1) | async-done | bytes 4194336 | tf_op jit(solution)/shard_map/all_to_all | solution.py:141
  211.0 6.6 all-to-all-start.3
  218.0 116.0 %all-gather.1 = s32[32,2,32]{2,1,0:T(2,128)S(1)} all-gather(s32[1,2,32]{2,1,0:T(2,128)S(1)} %bitcast.153), channel_id=2, replica_groups=mesh['pipe'=1,'expert'=32] {'expert'}, dimensions={0}, use_global_device_ids=true | all-gather | bytes 8448 | tf_op jit(solution)/shard_map/all_gather | solution.py:132
  337.7 10.9 %scatter_custom_fusion.6 = bf16[1024,2048]{1,0:T(8,128)(2,1)} fusion(s32[384]{0:T(512)S(1)} %fusion.61, bf16[]{:T(256)} %constant.139.clone.1, bf16[64,2048]{1,0:T(8,128)(2,1)S(1)} %get-tuple-element.164, s32[1024]{0:T(1024)S(1)} %pad_clamp_fusion.2), kind=kCustom, calls=%fused_computation.66 | custom fusion | bytes 4194306 | tf_op jit(solution)/shard_map/scatter | solution.py:62
  349.0 10.1 %scatter_custom_fusion.1 = bf16[1024,2048]{1,0:T(8,128)(2,1)} fusion(s32[1024]{0:T(1024)S(1)} %bitcast.156, bf16[1024,2048]{1,0:T(8,128)(2,1)} %bitcast.11, bf16[]{:T(256)} %constant.139.clone.1), kind=kCustom, calls=%fused_computation.76 | custom fusion | bytes 4194816 | tf_op jit(solution)/shard_map/scatter | solution.py:86
  359.1 10.1 %scatter_custom_fusion.3 = bf16[1024,2048]{1,0:T(8,128)(2,1)} fusion(s32[1024]{0:T(1024)S(1)} %bitcast.157, bf16[1024,2048]{1,0:T(8,128)(2,1)} %bitcast.15, bf16[]{:T(256)} %constant.139.clone.1), kind=kCustom, calls=%fused_computation.72 | custom fusion | bytes 4194816 | tf_op jit(solution)/shard_map/scatter | solution.py:81
  369.2 5.2 all-to-all-start.4
  374.4 2.5 broadcast.515.clone
  376.9 11.7 %while.25 = (s32[]{:T(128)}, bf16[1024,2048]{1,0:T(8,128)(2,1)}, bf16[1024]{0:T(1024)(128)(2,1)S(1)}, s32[]{:T(128)}, bf16[1024,2048]{1,0:T(8,128)(2,1)}, /*inde...) while((s32[]{:T(128)}, bf16[1024,2048]{1,0:T(8,128)(2,1)}, ...), condition=%wide.region_13.14_spmd, body=%wide.region_11.13_spmd.sunk | while | flops 4032102144 | bytes 69732112 | solution.py:106
  377.1 3.3 fusion.112
  380.4 2.3 fusion.113
  382.7 2.5 multiply_reduce_fusion.6
  388.6 11.6 %gather_fusion = bf16[1024,2048]{1,0:T(8,128)(2,1)} fusion(bf16[1024,2048]{1,0:T(8,128)(2,1)} %get-tuple-element.100, s32[1024]{0:T(1024)S(1)} %broadcast_clamp_fusion.1), kind=kCustom, calls=%fused_computation.2 | custom fusion | bytes 8392704 | tf_op jit(solution)/shard_map/gather | solution.py:108
  400.2 10.1 %scatter_custom_fusion.5 = bf16[1024,2048]{1,0:T(8,128)(2,1)} fusion(s32[1024]{0:T(1024)S(1)} %bitcast.154, bf16[1024,2048]{1,0:T(8,128)(2,1)} %bitcast.31, bf16[]{:T(256)} %constant.139.clone.1), kind=kCustom, calls=%fused_computation.68 | custom fusion | bytes 4194816 | tf_op jit(solution)/shard_map/scatter | solution.py:86
  410.3 4.5 broadcast_select_fusion.1
  414.7 51.1 %all-to-all-done.4 = bf16[32,32,2048]{2,1,0:T(8,128)(2,1)} async-done(((bf16[32,32,2048]{2,1,0:T(8,128)(2,1)}), bf16[32,32,2048]{2,1,0:T(8,128)(2,1)}, u32[]{:S(2)}, u32[]{:S(2)}) %all-to-all-start.4) | async-done | bytes 4194336 | tf_op jit(solution)/shard_map/all_to_all | solution.py:141
  465.8 7.0 all-to-all-start.2
  472.8 10.0 %scatter_custom_fusion.7 = bf16[1024,2048]{1,0:T(8,128)(2,1)} fusion(s32[1024]{0:T(1024)S(1)} %bitcast.155, bf16[1024,2048]{1,0:T(8,128)(2,1)} %bitcast.34, bf16[]{:T(256)} %constant.139.clone.1), kind=kCustom, calls=%fused_computation.64 | custom fusion | bytes 4194816 | tf_op jit(solution)/shard_map/scatter | solution.py:81
  482.8 2.5 broadcast.515.clone.1
  485.3 11.6 %while.26 = (s32[]{:T(128)}, bf16[1024,2048]{1,0:T(8,128)(2,1)}, bf16[1024]{0:T(1024)(128)(2,1)S(1)}, s32[]{:T(128)}, bf16[1024,2048]{1,0:T(8,128)(2,1)}, /*inde...) while((s32[]{:T(128)}, bf16[1024,2048]{1,0:T(8,128)(2,1)}, ...), condition=%wide.region_27.28_spmd, body=%wide.region_25.27_spmd.sunk | while | flops 4032102144 | bytes 69732112 | solution.py:106
  485.3 3.3 fusion.124
  488.7 2.3 fusion.125
  491.0 2.5 multiply_reduce_fusion.7
  494.6 2.1 fusion.127
  496.9 11.5 %gather_fusion.2 = bf16[1024,2048]{1,0:T(8,128)(2,1)} fusion(bf16[1024,2048]{1,0:T(8,128)(2,1)} %get-tuple-element.101, s32[1024]{0:T(1024)S(1)} %broadcast_clamp_fusion), kind=kCustom, calls=%fused_computation.6 | custom fusion | bytes 8392704 | tf_op jit(solution)/shard_map/gather | solution.py:108
  508.4 4.5 broadcast_select_fusion
  513.0 51.0 %all-to-all-done.2 = bf16[32,32,2048]{2,1,0:T(8,128)(2,1)} async-done(((bf16[32,32,2048]{2,1,0:T(8,128)(2,1)}), bf16[32,32,2048]{2,1,0:T(8,128)(2,1)}, u32[]{:S(2)}, u32[]{:S(2)}) %all-to-all-start.2) | async-done | bytes 4194336 | tf_op jit(solution)/shard_map/all_to_all | solution.py:148
  564.0 6.6 all-to-all-start.5
  570.8 7.1 gather_fusion.1
  577.9 2.2 reshape.911
  580.1 81.9 %all-to-all-done.5 = bf16[32,32,2048]{2,1,0:T(8,128)(2,1)} async-done(((bf16[32,32,2048]{2,1,0:T(8,128)(2,1)}), bf16[32,32,2048]{2,1,0:T(8,128)(2,1)}, u32[]{:S(2)}, u32[]{:S(2)}) %all-to-all-start.5) | async-done | bytes 4194336 | tf_op jit(solution)/shard_map/all_to_all | solution.py:148
  662.0 7.1 gather_fusion.3
  669.1 2.1 reshape.912
  671.3 3.9 multiply_reduce_fusion.3
  677.0 6.8 gather_fusion.4
  683.8 6.8 gather_fusion.6
  691.4 6.5 all-to-all-start.7
  698.6 5.3 all-to-all-done.7
  703.8 3.7 all-to-all-start.6
  707.7 2.8 gather_fusion.7
  710.7 2.8 all-to-all-done.6
  713.7 2.8 gather_fusion.5
  (139 shorter events, 19.2 us)
Async XLA Ops:
  4.4 17.3 %copy-start.10 = (s32[384]{0:T(512)}, s32[384]{0:T(512)S(1)}, u32[]{:S(2)}) copy-start(s32[384]{0:T(512)S(1)} %fusion.59) | copy-start | bytes 4612
  14.9 6.8 copy-start.2
  14.9 98.0 %all-to-all-start = ((bf16[32,32,2048]{2,1,0:T(8,128)(2,1)}), bf16[32,32,2048]{2,1,0:T(8,128)(2,1)}, u32[]{:S(2)}, u32[]{:S(2)}) async-start(bf16[32,32,2048]{2,1,0:T(8,128)(2,1)} %bitcast.143), calls=%async_computation | async-start | bytes 8388608 | tf_op jit(solution)/shard_map/all_to_all | solution.py:141
  112.9 98.1 %all-to-all-start.1 = ((bf16[32,32,2048]{2,1,0:T(8,128)(2,1)}), bf16[32,32,2048]{2,1,0:T(8,128)(2,1)}, u32[]{:S(2)}, u32[]{:S(2)}) async-start(bf16[32,32,2048]{2,1,0:T(8,128)(2,1)} %bitcast.142), calls=%async_computation.1 | async-start | bytes 8388608 | tf_op jit(solution)/shard_map/all_to_all | solution.py:141
  211.0 6.6 copy-start.3
  211.0 158.1 %all-to-all-start.3 = ((bf16[32,32,2048]{2,1,0:T(8,128)(2,1)}), bf16[32,32,2048]{2,1,0:T(8,128)(2,1)}, u32[]{:S(2)}, u32[]{:S(2)}) async-start(bf16[32,32,2048]{2,1,0:T(8,128)(2,1)} %bitcast.140), calls=%async_computation.3 | async-start | bytes 8388608 | tf_op jit(solution)/shard_map/all_to_all | solution.py:141
  334.2 2.5 copy-start.8
  334.2 2.2 copy-start.6
  334.2 2.5 copy-start.4
  369.2 96.6 %all-to-all-start.4 = ((bf16[32,32,2048]{2,1,0:T(8,128)(2,1)}), bf16[32,32,2048]{2,1,0:T(8,128)(2,1)}, u32[]{:S(2)}, u32[]{:S(2)}) async-start(bf16[32,32,2048]{2,1,0:T(8,128)(2,1)} %bitcast.141), calls=%async_computation.4 | async-start | bytes 8388608 | tf_op jit(solution)/shard_map/all_to_all | solution.py:141
  377.1 3.4 copy-start.13
  377.1 5.6 copy-start.15
  382.7 2.5 copy-start.17
  465.8 98.2 %all-to-all-start.2 = ((bf16[32,32,2048]{2,1,0:T(8,128)(2,1)}), bf16[32,32,2048]{2,1,0:T(8,128)(2,1)}, u32[]{:S(2)}, u32[]{:S(2)}) async-start(bf16[32,32,2048]{2,1,0:T(8,128)(2,1)} %broadcast_select_fusion.1), calls=%async_computation.2 | async-start | bytes 8388608 | tf_op jit(solution)/shard_map/all_to_all | solution.py:148
  485.3 3.3 copy-start.14
  485.3 5.6 copy-start.16
  491.0 2.5 copy-start.18
  513.0 57.6 %copy-start.12 = (f32[1,2,64,6]{2,1,3,0:T(2,128)S(1)}, f32[1,2,64,6]{2,1,3,0:T(2,128)}, u32[]{:S(2)}) copy-start(f32[1,2,64,6]{2,1,3,0:T(2,128)} %param.14) | copy-start | bytes 9220
  513.0 57.8 %copy-start.11 = (s32[384]{0:T(512)S(1)}, s32[384]{0:T(512)}, u32[]{:S(2)}) copy-start(s32[384]{0:T(512)} %copy-done.10) | copy-start | bytes 4612
  564.0 98.0 %all-to-all-start.5 = ((bf16[32,32,2048]{2,1,0:T(8,128)(2,1)}), bf16[32,32,2048]{2,1,0:T(8,128)(2,1)}, u32[]{:S(2)}, u32[]{:S(2)}) async-start(bf16[32,32,2048]{2,1,0:T(8,128)(2,1)} %broadcast_select_fusion), calls=%async_computation.5 | async-start | bytes 8388608 | tf_op jit(solution)/shard_map/all_to_all | solution.py:148
  671.3 3.9 copy-start
  671.3 5.4 copy-start.1
  676.7 14.0 %copy-start.5 = (s32[32]{0:T(128)S(1)}, s32[32]{0:T(128)}, u32[]{:S(2)}) copy-start(s32[32]{0:T(128)} %copy-done.4) | copy-start | bytes 388
  676.7 14.0 %copy-start.7 = (s32[32]{0:T(128)S(1)}, s32[32]{0:T(128)}, u32[]{:S(2)}) copy-start(s32[32]{0:T(128)} %copy-done.6) | copy-start | bytes 388
  676.7 14.0 %copy-start.9 = (s32[32]{0:T(128)S(1)}, s32[32]{0:T(128)}, u32[]{:S(2)}) copy-start(s32[32]{0:T(128)} %copy-done.8) | copy-start | bytes 388
  676.9 40.5 %collective-permute-start = (bf16[1,2,64,2048]{3,2,1,0:T(8,128)(2,1)S(1)}, bf16[1,2,64,2048]{3,2,1,0:T(8,128)(2,1)S(1)}, u32[]{:S(2)}, u32[]{:S(2)}) collective-permute-start(bf16[1,2,64,2048]{3,2,1,0:T(8,128)(2,1)S(1)} %pad_maximum_fusion), channel_id=1, source_target_pairs={{0,0},{1,1},{2,2},{3,3},{4,4},{5,5},{6,6},{7,7},{8,8},{9,9},{10,10... | collective-permute-start | bytes 1572872 | tf_op jit(solution)/shard_map/ppermute | solution.py:14
  691.4 12.4 %all-to-all-start.7 = ((bf16[32,1,32]{2,1,0:T(2,128)(2,1)}), bf16[32,1,32]{2,1,0:T(2,128)(2,1)S(1)}, u32[]{:S(2)}, u32[]{:S(2)}) async-start(bf16[32,1,32]{2,1,0:T(2,128)(2,1)} %copy.105), calls=%async_computation.7 | async-start | bytes 32768 | tf_op jit(solution)/shard_map/all_to_all | solution.py:148
  703.8 9.7 %all-to-all-start.6 = ((bf16[32,1,32]{2,1,0:T(2,128)(2,1)}), bf16[32,1,32]{2,1,0:T(2,128)(2,1)S(1)}, u32[]{:S(2)}, u32[]{:S(2)}) async-start(bf16[32,1,32]{2,1,0:T(2,128)(2,1)} %copy.104), calls=%async_computation.6 | async-start | bytes 32768 | tf_op jit(solution)/shard_map/all_to_all | solution.py:148
where the time goes:
time: 729 us; the launch traced here: 719 us
  waiting for transfers between devices  352 us (48%)
  local copies, waits for them, and re-layouts  157 us (22%)
  blocking collectives  116 us (16%)
  starting transfers between devices  49.2 us (7%)
  matrix products  22.6 us (3%)
  other arithmetic  19.2 us (3%)
    all_to_all x4, waiting for transfers between devices, send_each(): lax.all_to_all(shortened(pair), 'expert', split_axis=0, concat_axis=0, ti...  211 us
    all_to_all x4, waiting for transfers between devices, back_each(): lax.all_to_all(shortened(pair), 'expert', split_axis=0, concat_axis=0, ti...  141 us
    all_gather x1, blocking collectives, on_device(): table = lax.all_gather(local_counts[None], 'expert', axis=0, tiled=True)  116 us
    all_to_all x4, starting transfers between devices, send_each(): lax.all_to_all(shortened(pair), 'expert', split_axis=0, concat_axis=0, ti...  25.5 us
    all_to_all x4, starting transfers between devices, back_each(): lax.all_to_all(shortened(pair), 'expert', split_axis=0, concat_axis=0, ti...  23.7 us
    gather x2, local copies, waits for them, and re-layouts, expert_pass(): block_grads[source]  23.1 us
    scatter x2, local copies, waits for them, and re-layouts, expert_pass(): jnp.zeros((total, width), jnp.bfloat16).at[target].set(x_flat[token_of])  21.3 us
    scatter x2, local copies, waits for them, and re-layouts, expert_pass(): jnp.zeros((total, width), jnp.bfloat16).at[target].set(grad_flat[token_of])  20.9 us
  transfers between devices with their start and end apart: 9, of which 7 were waited for; matrix products, arithmetic and copies ran while one was open for 23% of the time, Pallas kernels for 0%

commit v1 on v0

v1 whole, which is shorter than its diff:
```python
import jax
import jax.numpy as jnp
from jax import lax
from jax.experimental import pallas as pl
from jax.experimental.pallas import tpu as pltpu
from jax.sharding import PartitionSpec as P


def expert_kernel(x_ref, g_ref, gate_ref, wgu_ref, wdt_ref, wgut_ref, out_ref, score_ref):
    hidden = wdt_ref.shape[1]
    pre = jnp.dot(x_ref[...], wgu_ref[...], preferred_element_type=jnp.float32)
    gate_pre = pre[:, :hidden]
    up_pre = pre[:, hidden:]
    back = jnp.dot(g_ref[...], wdt_ref[...], preferred_element_type=jnp.float32)
    logistic = 1.0 / (1.0 + jnp.exp(-gate_pre))
    swish = gate_pre * logistic
    d_up = back * swish
    score_ref[...] = jnp.sum(d_up * up_pre, axis=1, keepdims=True)
    d_gate = back * up_pre * logistic * (1.0 + gate_pre * (1.0 - logistic))
    both = jnp.concatenate([d_gate.astype(jnp.bfloat16), d_up.astype(jnp.bfloat16)], axis=1)
    pair = jnp.dot(both, wgut_ref[...], preferred_element_type=jnp.float32)
    pair = pair.astype(jnp.bfloat16).astype(jnp.float32)
    out_ref[...] = (gate_ref[...] * pair).astype(jnp.bfloat16)


def expert_all(x, g, gate, wgu, wdt, wgut):
    rows, width = x.shape
    hidden = wdt.shape[1]
    block = min(512, rows)
    whole = lambda a: pl.BlockSpec(a.shape, lambda i: (0, 0), pipeline_mode=pl.Buffered(1))
    part = lambda cols: pl.BlockSpec((block, cols), lambda i: (i, 0))
    return pl.pallas_call(
        expert_kernel,
        grid=(rows // block,),
        in_specs=[part(width), part(width), part(1), whole(wgu), whole(wdt), whole(wgut)],
        out_specs=[part(width), part(1)],
        out_shape=[
            jax.ShapeDtypeStruct((rows, width), jnp.bfloat16),
            jax.ShapeDtypeStruct((rows, 1), jnp.float32),
        ],
        compiler_params=pltpu.CompilerParams(vmem_limit_bytes=56 * 1024 * 1024),
        cost_estimate=pl.CostEstimate(
            flops=10 * rows * width * hidden,
            bytes_accessed=rows * width * 6 + 10 * width * hidden,
            transcendentals=rows * hidden,
        ),
    )(x, g, gate, wgu, wdt, wgut)


def on_device(inputs, grads_out, expert_ids, gate_values, w_gate, w_up, w_down):
    experts = lax.axis_size("expert")
    x_all, grad_all = inputs[0], grads_out[0]
    ids_all, gates_all = expert_ids[0], gate_values[0]
    micro_count, rows, width = x_all.shape
    onehot = ids_all[:, :, :, None] == jnp.arange(experts, dtype=jnp.int32)
    dense = jnp.sum(jnp.where(onehot, gates_all[..., None], 0.0), axis=2)
    dense = jnp.transpose(dense, (2, 0, 1))
    dense = lax.all_to_all(dense, "expert", split_axis=0, concat_axis=0, tiled=True)
    wgu = jnp.concatenate([w_gate[0, 0], w_up[0, 0]], axis=1)
    wgut = wgu.T
    wdt = w_down[0, 0].T
    delivered, scores = [], []
    gathered = []
    for micro in range(micro_count):
        gathered.append(
            (
                lax.all_gather(x_all[micro], "expert", axis=0, tiled=True),
                lax.all_gather(grad_all[micro], "expert", axis=0, tiled=True),
            )
        )
    for micro in range(micro_count):
        x, g = gathered[micro]
        out, score = expert_all(x, g, dense[:, micro].reshape(-1, 1), wgu, wdt, wgut)
        total = lax.psum_scatter(out, "expert", scatter_dimension=0, tiled=True)
        delivered.append(
            (grad_all[micro].astype(jnp.float32) + total.astype(jnp.float32)).astype(jnp.bfloat16)
        )
        scores.append(score.reshape(experts, rows).astype(jnp.bfloat16))
    back = lax.all_to_all(
        jnp.stack(scores, axis=1), "expert", split_axis=0, concat_axis=0, tiled=True
    )
    back = jnp.transpose(back, (1, 2, 0)).astype(jnp.float32)
    gate_grad = jnp.sum(jnp.where(onehot, back[:, :, None, :], 0.0), axis=3)
    received = jnp.stack(delivered)[None]
    count = lax.axis_size("pipe")
    received = lax.ppermute(received, "pipe", [(s, (s - 1) % count) for s in range(count)])
    return (received, gate_grad[None])


def solution(mesh):
    tokens = P("pipe", None, "expert", None)
    weights = P("pipe", "expert", None, None)
    return jax.shard_map(
        on_device,
        mesh=mesh,
        in_specs=(tokens,) * 4 + (weights,) * 3,
        out_specs=(tokens, tokens),
        check_vma=False,
    )
```

time: 729 us -> 644 us (0.88); the launches traced: 719 us -> 641 us
  local copies, waits for them, and re-layouts: 157 us -> 32.9 us
  waiting for transfers between devices: 352 us -> 454 us
  Pallas kernels: 0 us -> 96 us
  blocking collectives: 116 us -> 26.1 us
  starting transfers between devices: 49.2 us -> 6.5 us
  matrix products: 22.6 us -> 0 us
  between operations: 2.88 us -> 14.2 us
  other arithmetic: 19.2 us -> 11.6 us
    all_to_all x8 -> x1, waiting for transfers between devices: 352 us -> 0.01 us  [on_device(): lax.all_to_all(dense, 'expert', split_axis=0, concat_axis=0, tiled=True)]
    reduce_scatter x0 -> x2, waiting for transfers between devices: none -> 229 us  [on_device(): total = lax.psum_scatter(out, 'expert', scatter_dimension=0, tiled=True)]
    all_gather x0 -> x4, waiting for transfers between devices: none -> 224 us  [the longest x2 158 us: on_device(): lax.all_gather(grad_all[micro], 'expert', axis=0, tiled=True)]
    all_gather x1 -> x0, blocking collectives: 116 us -> none  [on_device(): table = lax.all_gather(local_counts[None], 'expert', axis=0, tiled=True)]
    pallas_call x0 -> x2, Pallas kernels: none -> 96 us  [expert_all(): pl.pallas_call(expert_kernel, grid=(rows // block,), in_specs=[part(width...]
    scatter x8 -> x0, local copies, waits for them, and re-layouts: 82.5 us -> none  [the longest x2 21.3 us: expert_pass(): jnp.zeros((total, width), jnp.bfloat16).at[target].set(x_flat[token_of])]
    gather x15 -> x0, local copies, waits for them, and re-layouts: 57 us -> none  [the longest x2 23.1 us: expert_pass(): block_grads[source]]
    all_to_all x8 -> x1, starting transfers between devices: 49.2 us -> 6.04 us  [on_device(): lax.all_to_all(dense, 'expert', split_axis=0, concat_axis=0, tiled=True)]
  transfers between devices with their start and end apart: 9 -> 8, of which waited for: 7 -> 6; matrix products, arithmetic and copies ran while one was open for 23% -> 6% of each run, Pallas kernels for 0% -> 15%
where the time goes in v1:
time: 644 us; the launch traced here: 641 us
  waiting for transfers between devices  454 us (70%)
  Pallas kernels  96 us (15%)
  local copies, waits for them, and re-layouts  32.9 us (5%)
  blocking collectives  26.1 us (4%)
  between operations  14.2 us (2%)
  other arithmetic  11.6 us (2%)
  starting transfers between devices  6.5 us (1%)
    reduce_scatter x2, waiting for transfers between devices, on_device(): total = lax.psum_scatter(out, 'expert', scatter_dimension=0, tiled=True)  229 us
    all_gather x2, waiting for transfers between devices, on_device(): lax.all_gather(grad_all[micro], 'expert', axis=0, tiled=True)  158 us
    pallas_call x2, Pallas kernels, expert_all(): pl.pallas_call(expert_kernel, grid=(rows // block,), in_specs=[part(width...  96 us
    all_gather x2, waiting for transfers between devices, on_device(): lax.all_gather(x_all[micro], 'expert', axis=0, tiled=True)  66.4 us
    all_to_all x1, blocking collectives, on_device(): lax.all_to_all(jnp.stack(scores, axis=1), 'expert', split_axis=0, concat_...  26.1 us
    unnamed x15, local copies, waits for them, and re-layouts  14.1 us
  transfers between devices with their start and end apart: 8, of which 6 were waited for; matrix products, arithmetic and copies ran while one was open for 6% of the time, Pallas kernels for 15%

profile of v1, /device:TPU:8, one launch (start us, length us, event | category | flops | bytes accessed | tf_op | source)
XLA Modules:
  0.0 641.4 jit_solution(13783975159491102812)
XLA Ops:
  7.2 0.0 all-gather.13.cloned.1.call-start
  7.2 1.9 fusion.6
  9.1 0.0 all-gather.13.cloned.1.call-update
  9.1 0.0 all-gather.15.cloned.1.call-start
  9.1 1.9 fusion.5
  11.0 0.0 all-gather.15.cloned.1.call-update
  11.1 0.0 all-gather.9.cloned.1.call-start
  11.1 0.7 all-gather.9.cloned.1.call-update
  11.8 0.0 all-gather.11.cloned.1.call-start
  11.8 0.5 all-gather.11.cloned.1.call-update
  12.4 0.7 copy.38
  13.1 0.7 copy.39
  13.8 0.7 reshape.59
  14.5 6.0 all-to-all-start
  20.6 0.0 reduce-scatter.5.cloned.1.call-start
  20.6 3.2 copy.41
  23.8 4.7 copy.42
  28.5 8.9 %fusion.4 = (bf16[1536,2048]{1,0:T(8,128)(2,1)}, bf16[2048,1536]{0,1:T(8,128)(2,1)}) fusion(bf16[2048,768]{0,1:T(8,128)(2,1)} %bitcast.30, bf16[2048,768]{0,1:T(8,128)(2,1)S(1)} %bitcast.29), kind=kLoop, calls=%fused_computation.17 | loop fusion | flops 12582912 | bytes 18874368 | tf_op jit(solution)/shard_map/transpose | solution.py:60
  37.5 8.9 %copy.45.wgu_ref = bf16[2048,1536]{1,0:T(8,128)(2,1)} copy(bf16[2048,1536]{0,1:T(8,128)(2,1)} %get-tuple-element.15) | data formatting | bytes 12582912 | tf_op jit(solution)/shard_map/concatenate | solution.py:59
  46.4 2.8 copy.43
  49.2 0.5 broadcast.9
  49.7 0.7 reduce.12
  50.4 0.1 reshape.60
  50.5 0.1 slice_reduce_fusion.1
  50.5 2.0 reshape_squeeze.9.gate_ref
  52.5 37.0 %all-gather.13.cloned.1.call-done = bf16[1,1,2048,2048]{3,2,1,0:T(8,128)(2,1)} async-done(((bf16[1,1,64,2048]{3,2,1,0:T(8,128)(2,1)}), bf16[1,1,2048,2048]{3,2,1,0:T(8,128)(2,1)}) %all-gather.13.cloned.1.call-update) | async-done | bytes 8388624 | tf_op jit(solution)/shard_map/all_gather | solution.py:67
  89.5 78.9 %all-gather.15.cloned.1.call-done = bf16[1,1,2048,2048]{3,2,1,0:T(8,128)(2,1)} async-done(((bf16[1,1,64,2048]{3,2,1,0:T(8,128)(2,1)}), bf16[1,1,2048,2048]{3,2,1,0:T(8,128)(2,1)}) %all-gather.15.cloned.1.call-update) | async-done | bytes 8388624 | tf_op jit(solution)/shard_map/all_gather | solution.py:68
  168.4 47.9 %shard_map.87 = (bf16[2048,2048]{1,0:T(8,128)(2,1)}, f32[2048,1]{1,0:T(8,128)}) custom-call(bf16[2048,2048]{1,0:T(8,128)(2,1)} %bitcast.38, bf16[2048,2048]{1,0:T(8,128)(2,1)} %bitcast.40, f32[2048,1]{1,0:T(8,128)} %reshape_squeeze.9.gate_ref, bf16[2048,1536]{1,0:T(8,128)(2,1)} %copy.45.wgu_ref, bf16[2048,768]{1,0:T(8,128)(2,1)} %bitcast.31, ...), custom_call_target="tpu_custom_call" | custom-call | flops 32212254720 | bytes 40894464 | tf_op jit(solution)/shard_map/pallas_call | solution.py:32
  216.3 0.0 reduce-scatter.5.cloned.1.call-update
  216.4 0.2 reduce-scatter.3.cloned.1.call-start
  216.6 2.0 reshape_squeeze.8.gate_ref
  218.6 29.4 %all-gather.9.cloned.1.call-done = bf16[1,1,2048,2048]{3,2,1,0:T(8,128)(2,1)} async-done(((bf16[1,1,64,2048]{3,2,1,0:T(8,128)(2,1)}), bf16[1,1,2048,2048]{3,2,1,0:T(8,128)(2,1)}) %all-gather.9.cloned.1.call-update) | async-done | bytes 8388624 | tf_op jit(solution)/shard_map/all_gather | solution.py:67
  248.0 78.8 %all-gather.11.cloned.1.call-done = bf16[1,1,2048,2048]{3,2,1,0:T(8,128)(2,1)} async-done(((bf16[1,1,64,2048]{3,2,1,0:T(8,128)(2,1)}), bf16[1,1,2048,2048]{3,2,1,0:T(8,128)(2,1)}) %all-gather.11.cloned.1.call-update) | async-done | bytes 8388624 | tf_op jit(solution)/shard_map/all_gather | solution.py:68
  326.7 48.1 %shard_map.86 = (bf16[2048,2048]{1,0:T(8,128)(2,1)}, f32[2048,1]{1,0:T(8,128)}) custom-call(bf16[2048,2048]{1,0:T(8,128)(2,1)} %bitcast.37, bf16[2048,2048]{1,0:T(8,128)(2,1)} %bitcast.39, f32[2048,1]{1,0:T(8,128)} %reshape_squeeze.8.gate_ref, bf16[2048,1536]{1,0:T(8,128)(2,1)} %copy.45.wgu_ref, bf16[2048,768]{1,0:T(8,128)(2,1)} %bitcast.32, ...), custom_call_target="tpu_custom_call" | custom-call | flops 32212254720 | bytes 40894464 | tf_op jit(solution)/shard_map/pallas_call | solution.py:32
  374.8 0.0 reduce-scatter.3.cloned.1.call-update
  374.9 1.2 copy-done.2
  376.1 0.3 convert_reduce_fusion
  376.4 82.0 %reduce-scatter.5.cloned.1.call-done = bf16[64,2048]{1,0:T(8,128)(2,1)} async-done(((bf16[2048,2048]{1,0:T(8,128)(2,1)}), bf16[64,2048]{1,0:T(8,128)(2,1)}) %reduce-scatter.5.cloned.1.call-update) | async-done | bytes 262160 | tf_op jit(solution)/shard_map/reduce_scatter | solution.py:74
  458.4 146.7 %reduce-scatter.3.cloned.1.call-done = bf16[64,2048]{1,0:T(8,128)(2,1)} async-done(((bf16[2048,2048]{1,0:T(8,128)(2,1)}), bf16[64,2048]{1,0:T(8,128)(2,1)}) %reduce-scatter.3.cloned.1.call-update) | async-done | bytes 262160 | tf_op jit(solution)/shard_map/reduce_scatter | solution.py:74
  605.2 1.2 fusion.2
  606.3 0.1 maximum_bitcast_fusion
  606.4 0.0 collective-permute-start
  606.4 0.3 convert_reduce_fusion.1
  606.8 0.1 convert_element_type.59
  606.9 0.1 convert_element_type.57
  607.0 26.1 %all_to_all.10 = bf16[32,2,64]{2,1,0:T(2,128)(2,1)S(1)} all-to-all(bf16[32,2,64]{2,1,0:T(2,128)(2,1)S(1)} %copy.48), channel_id=1, replica_groups=mesh['pipe'=1,'expert'=32] {'expert'}, dimensions={0} | all-to-all | bytes 16384 | tf_op jit(solution)/shard_map/all_to_all | solution.py:79
  633.1 0.6 copy.50
  633.8 0.8 copy.52
  (16 shorter events, 0.2 us)
Async XLA Ops:
  7.2 82.3 %all-gather.13.cloned.1.call-start = ((), (), s32[]{:S(2)}) async-start(), calls=%async_computation.8 | async-start | bytes 8650752 | tf_op jit(solution)/shard_map/all_gather | solution.py:67
  9.1 159.3 %all-gather.15.cloned.1.call-start = ((), (), s32[]{:S(2)}) async-start(), calls=%async_computation.9 | async-start | bytes 8650752 | tf_op jit(solution)/shard_map/all_gather | solution.py:68
  11.1 236.9 %all-gather.9.cloned.1.call-start = ((), (), s32[]{:S(2)}) async-start(), calls=%async_computation.6 | async-start | bytes 8650752 | tf_op jit(solution)/shard_map/all_gather | solution.py:67
  11.8 315.0 %all-gather.11.cloned.1.call-start = ((), (), s32[]{:S(2)}) async-start(), calls=%async_computation.7 | async-start | bytes 8650752 | tf_op jit(solution)/shard_map/all_gather | solution.py:68
  14.5 34.6 %all-to-all-start = ((f32[32,1,128]{2,1,0:T(1,128)}), f32[32,1,128]{2,1,0:T(1,128)S(1)}, u32[]{:S(2)}, u32[]{:S(2)}) async-start(f32[32,1,128]{2,1,0:T(1,128)} %reshape.59), calls=%async_computation | async-start | bytes 32768 | tf_op jit(solution)/shard_map/all_to_all | solution.py:58
  20.6 437.9 %reduce-scatter.5.cloned.1.call-start = ((), (), s32[]{:S(2)}) async-start(), calls=%async_computation.5 | async-start | bytes 8650752 | tf_op jit(solution)/shard_map/reduce_scatter | solution.py:74
  37.5 8.9 %copy-start = (bf16[1,1,768,2048]{3,2,1,0:T(8,128)(2,1)S(1)}, bf16[1,1,768,2048]{3,2,1,0:T(8,128)(2,1)}, u32[]{:S(2)}) copy-start(bf16[1,1,768,2048]{3,2,1,0:T(8,128)(2,1)} %param.13) | copy-start | bytes 9437188
  216.4 388.8 %reduce-scatter.3.cloned.1.call-start = ((), (), s32[]{:S(2)}) async-start(), calls=%async_computation.4 | async-start | bytes 8650752 | tf_op jit(solution)/shard_map/reduce_scatter | solution.py:74
  374.8 1.2 copy-start.2
  374.8 230.3 %copy-start.1 = (bf16[1,2,64,2048]{3,2,1,0:T(8,128)(2,1)S(1)}, bf16[1,2,64,2048]{3,2,1,0:T(8,128)(2,1)}, u32[]{:S(2)}) copy-start(bf16[1,2,64,2048]{3,2,1,0:T(8,128)(2,1)} %param.8) | copy-start | bytes 1572868
  374.8 231.6 %copy-start.3 = (f32[2048,1]{1,0:T(8,128)S(1)}, f32[2048,1]{1,0:T(8,128)}, u32[]{:S(2)}) copy-start(f32[2048,1]{1,0:T(8,128)} %get-tuple-element.8) | copy-start | bytes 24580
  606.4 27.4 %collective-permute-start = (bf16[1,2,64,2048]{3,2,1,0:T(8,128)(2,1)S(1)}, bf16[1,2,64,2048]{3,2,1,0:T(8,128)(2,1)S(1)}, u32[]{:S(2)}, u32[]{:S(2)}) collective-permute-start(bf16[1,2,64,2048]{3,2,1,0:T(8,128)(2,1)S(1)} %maximum_bitcast_fusion), channel_id=1, source_target_pairs={{0,0},{1,1},{2,2},{3,3},{4,4},{5,5},{6,6},{7,7},{8,8},{9,9},{10,10... | collective-permute-start | bytes 1572872 | tf_op jit(solution)/shard_map/ppermute | solution.py:86
Sparse Core Ops, SparseCore 0:
  10.9 78.5 all-gather.12
  92.4 76.0 all-gather.14
  171.9 76.0 all-gather.8
  250.7 76.0 all-gather.10
  328.9 129.5 reduce-scatter.4
  460.6 144.5 reduce-scatter.2

commit v2 on v1

v2 whole, which is shorter than its diff:
```python
import functools

import jax
import jax.numpy as jnp
from jax import lax
from jax.experimental import pallas as pl
from jax.experimental.pallas import tpu as pltpu
from jax.sharding import PartitionSpec as P

LANES = 128
NT = (((1,), (1,)), ((), ()))


def across(value, step, bits):
    total, scale = 0, 1
    for _ in range(bits):
        total = total + scale * (((value // scale) % 2 + (step // scale) % 2) % 2)
        scale = 2 * scale
    return total


def section_kernel(
    layers, payload, wg_hbm, wu_hbm, wd_hbm,
    out_ref, score_ref, gathered,
    wg, wu, wd, xv, acc, staged, plane_in, layer_out, layer_in,
    w_loc, w_send, w_recv, loc, z_send, z_recv, a_send, a_recv, f_send, f_recv,
    r_send, r_recv, l_send, l_recv,
):
    bits = layers.bit_length() - 1
    me = lax.axis_index("expert")
    z, place = me // 8, me % 8
    y, x, core = place // 4, (place // 2) % 2, place % 2

    def at(layer, row, column, side):
        return ((layer * 2 + row) * 2 + column) * 2 + side

    partner = at(z, y, x, 1 - core)
    peers = [at(z, y, 1 - x, core), at(z, 1 - y, x, core), at(z, 1 - y, 1 - x, core)]

    def layer_peer(step):
        return at(across(z, step, bits), y, x, core)

    def remote(src, dst, send, recv, device):
        return pltpu.make_async_remote_copy(
            src_ref=src, dst_ref=dst, send_sem=send, recv_sem=recv,
            device_id={"expert": device}, device_id_type=pl.DeviceIdType.MESH,
        )

    rows = payload.shape[1]
    width = out_ref.shape[1]
    many = 4 * rows

    def weight_copy(i):
        return remote(
            (wg_hbm, wu_hbm, wd_hbm)[i], (wg, wu, wd)[i].at[1], w_send.at[i], w_recv.at[i], partner
        )

    def weight_local(i):
        return pltpu.make_async_copy(
            (wg_hbm, wu_hbm, wd_hbm)[i], (wg, wu, wd)[i].at[0], w_loc.at[i]
        )

    def layer_gather(step):
        return remote(
            payload, gathered.at[step, 0], z_send.at[step], z_recv.at[step], layer_peer(step)
        )

    def plane_gather(step, side):
        return remote(
            gathered.at[step, 0], gathered.at[step, 1 + side],
            a_send.at[step, side], a_recv.at[step, side], peers[side],
        )

    def forward(step, side):
        return remote(
            gathered.at[step, 1 + side, side], gathered.at[step, 3, side],
            f_send.at[step, side], f_recv.at[step, side], peers[1 - side],
        )

    def plane_reduce(step, k):
        return remote(
            staged.at[step % 2, 1 + k], plane_in.at[step, k],
            r_send.at[step, k], r_recv.at[step, k], peers[k],
        )

    def layer_reduce(step):
        return remote(
            layer_out.at[step], layer_in.at[step], l_send.at[step], l_recv.at[step],
            layer_peer(step),
        )

    barrier = pltpu.get_barrier_semaphore()
    greeted = [partner] + peers + [layer_peer(s) for s in range(1, layers)]
    for device in greeted:
        pl.semaphore_signal(
            barrier, inc=1, device_id={"expert": device}, device_id_type=pl.DeviceIdType.MESH
        )
    first = pltpu.make_async_copy(payload, gathered.at[0, 0], loc.at[0])
    first.start()
    first.wait()
    for i in range(3):
        weight_local(i).start()
    pl.semaphore_wait(barrier, len(greeted))

    for side in range(2):
        plane_gather(0, side).start()
    if layers > 1:
        layer_gather(1).start()
    for i in range(3):
        weight_copy(i).start()
    for side in range(2):
        plane_gather(0, side).wait_recv()
        forward(0, side).start()

    lane = lax.broadcasted_iota(jnp.int32, (many, LANES), 1)

    def expert(j, expert_id, slot):
        xs = xv[:, 0, :, :width].reshape(many, width)
        gs = xv[:, 1, :, :width].reshape(many, width)
        gate_pre = jnp.dot(xs, wg[j], preferred_element_type=jnp.float32)
        up_pre = jnp.dot(xs, wu[j], preferred_element_type=jnp.float32)
        back = lax.dot_general(gs, wd[j], NT, preferred_element_type=jnp.float32)
        logistic = 1.0 / (1.0 + jnp.exp(-gate_pre))
        swish = gate_pre * logistic
        d_up = back * swish
        score = jnp.sum(d_up * up_pre, axis=1, keepdims=True)
        d_gate = (back * up_pre * logistic * (1.0 + gate_pre * (1.0 - logistic)))
        d_gate, d_up = d_gate.astype(jnp.bfloat16), d_up.astype(jnp.bfloat16)
        gates = xv[:, :, :, width:].astype(jnp.float32)
        gates = (gates[:, 0] + gates[:, 1]).reshape(many, LANES)
        gate = jnp.sum(jnp.where(lane == expert_id, gates, 0.0), axis=1, keepdims=True)
        spread = jnp.where(lane == expert_id, score, 0.0)
        tile = min(512, width)
        for col in range(0, width, tile):
            cols = pl.ds(col, tile)
            pair = lax.dot_general(d_gate, wg[j, cols, :], NT, preferred_element_type=jnp.float32)
            pair = pair + lax.dot_general(
                d_up, wu[j, cols, :], NT, preferred_element_type=jnp.float32
            )
            pair = gate * pair.astype(jnp.bfloat16).astype(jnp.float32)
            if j == 0:
                acc[:, cols] = pair
            else:
                staged[slot, :, :, cols] = (
                    (acc[:, cols] + pair).astype(jnp.bfloat16).reshape(4, rows, tile)
                )
        cols = pl.ds(width, LANES)
        if j == 0:
            acc[:, cols] = spread
        else:
            staged[slot, :, :, cols] = (
                (acc[:, cols] + spread).astype(jnp.bfloat16).reshape(4, rows, LANES)
            )

    def finish_plane(step):
        for k in range(3):
            plane_reduce(step, k).wait_send()
            plane_reduce(step, k).wait_recv()
        total = staged[step % 2, 0].astype(jnp.float32)
        for k in range(3):
            total = total + plane_in[step, k].astype(jnp.float32)
        layer_out[step] = total.astype(jnp.bfloat16)

        @pl.when(step > 0)
        def _():
            layer_reduce(step).start()

    def one_step(step, carry):
        @pl.when(step + 1 < layers)
        def _():
            layer_gather(step + 1).wait_recv()
            for side in range(2):
                plane_gather(step + 1, side).start()

        @pl.when(step + 2 < layers)
        def _():
            layer_gather(step + 2).start()

        for side in range(2):
            forward(step, side).wait_recv()
        load = pltpu.make_async_copy(gathered.at[step], xv, loc.at[1])
        load.start()
        load.wait()

        @pl.when(step == 0)
        def _():
            for i in range(3):
                weight_local(i).wait()

        expert(0, me, step % 2)

        @pl.when(step + 1 < layers)
        def _():
            for side in range(2):
                plane_gather(step + 1, side).wait_recv()
                forward(step + 1, side).start()

        @pl.when(step == 0)
        def _():
            for i in range(3):
                weight_copy(i).wait_recv()

        expert(1, partner, step % 2)
        for k in range(3):
            plane_reduce(step, k).start()

        @pl.when(step > 0)
        def _():
            finish_plane(step - 1)

        return carry

    lax.fori_loop(0, layers, one_step, 0)
    finish_plane(layers - 1)

    total = layer_out[0].astype(jnp.float32)
    for step in range(1, layers):
        layer_reduce(step).wait_recv()
        total = total + layer_in[step].astype(jnp.float32)
    own = xv.at[0, 1]
    grads = pltpu.make_async_copy(payload.at[1], own, loc.at[0])
    grads.start()
    grads.wait()
    out_ref[...] = (own[:, :width].astype(jnp.float32) + total[:, :width]).astype(jnp.bfloat16)
    score_ref[...] = total[:, width:].astype(jnp.bfloat16)

    for i in range(3):
        weight_copy(i).wait_send()
    for step in range(layers):
        for side in range(2):
            plane_gather(step, side).wait_send()
            forward(step, side).wait_send()
        if step > 0:
            layer_gather(step).wait_send()
            layer_reduce(step).wait_send()


def section(payload, w_gate, w_up, w_down, experts):
    layers = experts // 8
    _, rows, wide = payload.shape
    width, hidden = w_gate.shape
    bf16 = jnp.bfloat16
    sem = pltpu.SemaphoreType.DMA
    anywhere = pl.BlockSpec(memory_space=pl.ANY)
    vmem = pl.BlockSpec(memory_space=pltpu.VMEM)
    out, score, _ = pl.pallas_call(
        functools.partial(section_kernel, layers),
        in_specs=[anywhere] * 4,
        out_specs=[vmem, vmem, anywhere],
        out_shape=[
            jax.ShapeDtypeStruct((rows, width), bf16),
            jax.ShapeDtypeStruct((rows, LANES), bf16),
            jax.ShapeDtypeStruct((layers, 4, 2, rows, wide), bf16),
        ],
        scratch_shapes=[
            pltpu.VMEM((2, width, hidden), bf16),
            pltpu.VMEM((2, width, hidden), bf16),
            pltpu.VMEM((2, hidden, width), bf16),
            pltpu.VMEM((4, 2, rows, wide), bf16),
            pltpu.VMEM((4 * rows, wide), jnp.float32),
            pltpu.VMEM((2, 4, rows, wide), bf16),
            pltpu.VMEM((layers, 3, rows, wide), bf16),
            pltpu.VMEM((layers, rows, wide), bf16),
            pltpu.VMEM((layers, rows, wide), bf16),
            sem((3,)), sem((3,)), sem((3,)), sem((2,)),
            sem((layers,)), sem((layers,)),
            sem((layers, 2)), sem((layers, 2)),
            sem((layers, 2)), sem((layers, 2)),
            sem((layers, 3)), sem((layers, 3)),
            sem((layers,)), sem((layers,)),
        ],
        compiler_params=pltpu.CompilerParams(
            collective_id=0, has_side_effects=True, vmem_limit_bytes=63 * 1024 * 1024
        ),
    )(payload, w_gate, w_up, w_down)
    return out, score


def on_device(inputs, grads_out, expert_ids, gate_values, w_gate, w_up, w_down):
    experts = lax.axis_size("expert")
    x_all, grad_all = inputs[0], grads_out[0]
    micro, rows, width = x_all.shape
    count = micro * rows
    picks = expert_ids.shape[3]
    ids = expert_ids.reshape(count, picks)
    gates = gate_values.reshape(count, picks)
    onehot = ids[:, :, None] == jnp.arange(LANES, dtype=jnp.int32)
    dense = jnp.sum(jnp.where(onehot, gates[..., None], 0.0), axis=1)
    high = lax.reduce_precision(dense, 8, 7)
    low = (dense - high).astype(jnp.bfloat16)
    payload = jnp.stack(
        [
            jnp.concatenate([x_all.reshape(count, width), high.astype(jnp.bfloat16)], axis=1),
            jnp.concatenate([grad_all.reshape(count, width), low], axis=1),
        ]
    )
    out, score = section(payload, w_gate[0, 0], w_up[0, 0], w_down[0, 0], experts)
    gate_grad = jnp.sum(jnp.where(onehot, score.astype(jnp.float32)[:, None, :], 0.0), axis=2)
    received = out.reshape(1, micro, rows, width)
    sections = lax.axis_size("pipe")
    if sections > 1:
        received = lax.ppermute(
            received, "pipe", [(s, (s - 1) % sections) for s in range(sections)]
        )
    return (received, gate_grad.reshape(1, micro, rows, picks))


def solution(mesh):
    tokens = P("pipe", None, "expert", None)
    weights = P("pipe", "expert", None, None)
    return jax.shard_map(
        on_device,
        mesh=mesh,
        in_specs=(tokens,) * 4 + (weights,) * 3,
        out_specs=(tokens, tokens),
        check_vma=False,
    )
```

time: 644 us -> 314 us (0.49)
  waiting for transfers between devices: 454 us -> 0 us
  Pallas kernels: 96 us -> 305 us
  local copies, waits for them, and re-layouts: 32.9 us -> 4.1 us
  blocking collectives: 26.1 us -> 0 us
  between operations: 14.2 us -> 0.66 us
  other arithmetic: 11.6 us -> 3.79 us
  starting transfers between devices: 6.5 us -> 0 us
    reduce_scatter x2 -> x0, waiting for transfers between devices: 229 us -> none  [on_device(): total = lax.psum_scatter(out, 'expert', scatter_dimension=0, tiled=True)]
    all_gather x4 -> x0, waiting for transfers between devices: 224 us -> none  [the longest x2 158 us: on_device(): lax.all_gather(grad_all[micro], 'expert', axis=0, tiled=True)]
    pallas_call x2 -> x1, Pallas kernels: 96 us -> 305 us  [section(): pl.pallas_call(functools.partial(section_kernel, layers), in_specs=[anywh...]
    all_to_all x1 -> x0, blocking collectives: 26.1 us -> none  [on_device(): lax.all_to_all(jnp.stack(scores, axis=1), 'expert', split_axis=0, concat_...]
    unnamed x15 -> x1, local copies, waits for them, and re-layouts: 14.1 us -> 1.88 us
    transpose x1 -> x0, other arithmetic: 8.92 us -> none  [on_device(): wgut = wgu.T]
    concatenate x1 -> x0, local copies, waits for them, and re-layouts: 8.9 us -> none  [on_device(): wgu = jnp.concatenate([w_gate[0, 0], w_up[0, 0]], axis=1)]
  transfers between devices with their start and end apart: 8 -> 0, of which waited for: 6 -> 0; matrix products, arithmetic and copies ran while one was open for 6% -> 0% of each run, Pallas kernels for 15% -> 0%
where the time goes in v2:
time: 314 us
  Pallas kernels  305 us (97%)
  local copies, waits for them, and re-layouts  4.1 us (1%)
  other arithmetic  3.79 us (1%)
    pallas_call x1, Pallas kernels, section(): pl.pallas_call(functools.partial(section_kernel, layers), in_specs=[anywh...  305 us

profile of v2, /device:TPU:8, one launch (start us, length us, event | category | flops | bytes accessed | tf_op | source)
XLA Modules:
  0.0 313.9 jit_solution(1470710914923304784)
XLA Ops:
  0.6 0.8 eq.15
  1.4 0.8 broadcast_in_dim.26
  2.2 0.3 select_reduce_fusion.1
  2.5 1.3 maximum_bitcast_fusion
  3.8 1.1 pad_maximum_fusion.payload
  4.9 305.4 %shard_map.86 = (bf16[128,2048]{1,0:T(8,128)(2,1)}, bf16[128,128]{1,0:T(8,128)(2,1)}, bf16[4,4,2,128,2176]{4,3,2,1,0:T(8,128)(2,1)}) custom-call(bf16[2,128,2176]{2,1,0:T(8,128)(2,1)} %pad_maximum_fusion.payload, bf16[2048,768]{1,0:T(8,128)(2,1)} %bitcast.16, bf16[2048,768]{1,0:T(8,128)(2,1)} %bitcast.17, bf16[768,2048]{1,0:T(8,128)(2,1)} %bitcast.18), custom_call_target="tpu_custom_call" | custom-call | tf_op jit(solution)/shard_map/pallas_call | solution.py:246
  310.3 0.8 convert_element_type.11
  311.1 0.3 select_reduce_fusion
  311.4 0.7 reshape.14
  312.0 1.9 copy.12
  (1 shorter events, 0.0 us)

commit v3 on v2

--- a/solution.py
+++ b/solution.py
@@ -22,7 +22,7 @@
 def section_kernel(
     layers, payload, wg_hbm, wu_hbm, wd_hbm,
     out_ref, score_ref, gathered,
-    wg, wu, wd, xv, acc, staged, plane_in, layer_out, layer_in,
+    wg, wu, wd, xv, acc, staged, plane_in, diag_in, layer_out, layer_in,
     w_loc, w_send, w_recv, loc, z_send, z_recv, a_send, a_recv, f_send, f_recv,
     r_send, r_recv, l_send, l_recv,
 ):
@@ -49,6 +49,7 @@
     rows = payload.shape[1]
     width = out_ref.shape[1]
     many = 4 * rows
+    half = rows // 2
 
     def weight_copy(i):
         return remote(
@@ -81,6 +82,12 @@
         return remote(
             staged.at[step % 2, 1 + k], plane_in.at[step, k],
             r_send.at[step, k], r_recv.at[step, k], peers[k],
+        )
+
+    def diag_reduce(step, side):
+        return remote(
+            staged.at[step % 2, 3, pl.ds(side * half, half)], diag_in.at[step, side],
+            r_send.at[step, 2 + side], r_recv.at[step, 2 + side], peers[side],
         )
 
     def layer_reduce(step):
@@ -152,12 +159,23 @@
                 (acc[:, cols] + spread).astype(jnp.bfloat16).reshape(4, rows, LANES)
             )
 
+    def merge_plane(step):
+        for side in range(2):
+            diag_reduce(step, side).wait_send()
+            diag_reduce(step, side).wait_recv()
+            part = pl.ds(side * half, half)
+            merged = staged[step % 2, 2 - side, part].astype(jnp.float32)
+            merged = merged + diag_in[step, side].astype(jnp.float32)
+            staged[step % 2, 2 - side, part] = merged.astype(jnp.bfloat16)
+        for k in range(2):
+            plane_reduce(step, k).start()
+
     def finish_plane(step):
-        for k in range(3):
+        for k in range(2):
             plane_reduce(step, k).wait_send()
             plane_reduce(step, k).wait_recv()
         total = staged[step % 2, 0].astype(jnp.float32)
-        for k in range(3):
+        for k in range(2):
             total = total + plane_in[step, k].astype(jnp.float32)
         layer_out[step] = total.astype(jnp.bfloat16)
 
@@ -200,17 +218,24 @@
             for i in range(3):
                 weight_copy(i).wait_recv()
 
+        @pl.when(step > 1)
+        def _():
+            finish_plane(step - 2)
+
+        @pl.when(step > 0)
+        def _():
+            merge_plane(step - 1)
+
         expert(1, partner, step % 2)
-        for k in range(3):
-            plane_reduce(step, k).start()
-
-        @pl.when(step > 0)
-        def _():
-            finish_plane(step - 1)
+        for side in range(2):
+            diag_reduce(step, side).start()
 
         return carry
 
     lax.fori_loop(0, layers, one_step, 0)
+    if layers > 1:
+        finish_plane(layers - 2)
+    merge_plane(layers - 1)
     finish_plane(layers - 1)
 
     total = layer_out[0].astype(jnp.float32)
@@ -259,14 +284,15 @@
             pltpu.VMEM((4, 2, rows, wide), bf16),
             pltpu.VMEM((4 * rows, wide), jnp.float32),
             pltpu.VMEM((2, 4, rows, wide), bf16),
-            pltpu.VMEM((layers, 3, rows, wide), bf16),
+            pltpu.VMEM((layers, 2, rows, wide), bf16),
+            pltpu.VMEM((layers, 2, rows // 2, wide), bf16),
             pltpu.VMEM((layers, rows, wide), bf16),
             pltpu.VMEM((layers, rows, wide), bf16),
             sem((3,)), sem((3,)), sem((3,)), sem((2,)),
             sem((layers,)), sem((layers,)),
             sem((layers, 2)), sem((layers, 2)),
             sem((layers, 2)), sem((layers, 2)),
-            sem((layers, 3)), sem((layers, 3)),
+            sem((layers, 4)), sem((layers, 4)),
             sem((layers,)), sem((layers,)),
         ],
         compiler_params=pltpu.CompilerParams(

time: 314 us -> 296 us (0.943)
  Pallas kernels: 305 us -> 287 us
    pallas_call x1, Pallas kernels: 305 us -> 287 us  [section(): pl.pallas_call(functools.partial(section_kernel, layers), in_specs=[anywh...]
where the time goes in v3:
time: 296 us
  Pallas kernels  287 us (97%)
  local copies, waits for them, and re-layouts  4.1 us (1%)
  other arithmetic  3.79 us (1%)
    pallas_call x1, Pallas kernels, section(): pl.pallas_call(functools.partial(section_kernel, layers), in_specs=[anywh...  287 us

profile of v3, /device:TPU:8, one launch (start us, length us, event | category | flops | bytes accessed | tf_op | source)
XLA Modules:
  0.0 295.7 jit_solution(2375985837601684658)
XLA Ops:
  0.6 0.8 eq.15
  1.4 0.8 broadcast_in_dim.26
  2.2 0.3 select_reduce_fusion.1
  2.5 1.3 maximum_bitcast_fusion
  3.8 1.1 pad_maximum_fusion.payload
  4.9 287.1 %shard_map.86 = (bf16[128,2048]{1,0:T(8,128)(2,1)}, bf16[128,128]{1,0:T(8,128)(2,1)}, bf16[4,4,2,128,2176]{4,3,2,1,0:T(8,128)(2,1)}) custom-call(bf16[2,128,2176]{2,1,0:T(8,128)(2,1)} %pad_maximum_fusion.payload, bf16[2048,768]{1,0:T(8,128)(2,1)} %bitcast.16, bf16[2048,768]{1,0:T(8,128)(2,1)} %bitcast.17, bf16[768,2048]{1,0:T(8,128)(2,1)} %bitcast.18), custom_call_target="tpu_custom_call" | custom-call | tf_op jit(solution)/shard_map/pallas_call | solution.py:271
  292.0 0.8 convert_element_type.11
  292.8 0.3 select_reduce_fusion
  293.1 0.7 reshape.14
  293.8 1.9 copy.12
  (1 shorter events, 0.0 us)
